TPU v7x, 32 devices: a whole 2x2x4 slice. The times are simulated.
32 devices in a mesh: vec: 8 (over z, core), rep: 4 (over y, x).
Axes of the slice: x: 2, y: 2, z: 4, core: 2. Of those that a mesh axis runs over, the one named last changes fastest.
Arguments:
- vectors: bfloat16 [1024, 1024], P('vec'), may hold values from 0 to 2
- pivot_index: int32 [4, 8], P('rep'), may hold values from 0 to 1023
Outputs:
- similarity: bfloat16 [7, 32, 1024, 128], P(None, 'rep', 'vec')
All inputs are finite; a program needn't handle non-finite values.
Results may differ from a plain program's by a relative error of at most 0.011.
Values may be sent and summed in bfloat16 or wider, within the bound.
A program may use at most 64 MiB of HBM per device.

v0:
```python
import math
import jax
import jax.numpy as jnp
from jax import lax
from jax.sharding import PartitionSpec as P

HALF = 3


def from_behind(block, axis, distance):
    devices = range(lax.axis_size(axis))
    route = [((i - distance) % len(devices), i) for i in devices]
    return lax.ppermute(block, axis, route)


def contract(left, right):
    return lax.dot_general(
        left, right, (((1,), (1,)), ((), ())), preferred_element_type=jnp.float32
    )


def on_device(vectors, pivot_index):
    block_rows, fields = vectors.shape
    position = lax.axis_index("vec")
    wanted = pivot_index.reshape(-1) - position * block_rows
    columns = jnp.arange(block_rows, dtype=jnp.int32)
    onehot = (wanted[:, None] == columns[None, :]).astype(jnp.bfloat16)
    local_rows = jnp.dot(onehot, vectors, preferred_element_type=jnp.float32)
    pivots = lax.psum(local_rows, "vec")
    count = pivots.shape[0]
    centre = jnp.sum(pivots, axis=1) / fields
    scaled = (vectors.astype(jnp.float32)[None, :, :] * pivots[:, None, :]).astype(jnp.bfloat16)
    scaled = scaled.reshape(count * block_rows, fields)
    replicas = lax.axis_size("rep")
    share = block_rows // replicas
    own_rows = lax.dynamic_slice_in_dim(vectors, lax.axis_index("rep") * share, share, 0)
    window = 2 * HALF + 1
    triples = [None] * window
    grams = [None] * window
    triples[HALF] = contract(scaled, vectors)
    grams[HALF] = contract(own_rows, vectors)
    lower = vectors
    upper = vectors
    for reach in range(1, HALF + 1):
        lower = from_behind(lower, "vec", 1)
        upper = from_behind(upper, "vec", -1)
        triples[HALF - reach] = contract(scaled, lower)
        grams[HALF - reach] = contract(own_rows, lower)
        triples[HALF + reach] = contract(scaled, upper)
        grams[HALF + reach] = contract(own_rows, upper)
    triple_all = jnp.stack(triples).reshape(window, count, block_rows, block_rows)
    gram_all = jnp.stack(grams)
    gram_all = lax.all_gather(gram_all, "rep", axis=1, tiled=True)
    similarity = (triple_all - centre[None, :, None, None] * gram_all[:, None, :, :]) / math.sqrt(
        fields
    )
    return similarity.astype(jnp.bfloat16)


def solution(mesh):
    in_specs = (P("vec", None), P("rep", None))
    out_specs = P(None, "rep", "vec", None)
    return jax.shard_map(
        on_device, mesh=mesh, in_specs=in_specs, out_specs=out_specs, check_vma=False
    )
```

profile of v0, /device:TPU:0, one launch (start us, length us, event | category | flops | bytes accessed | tf_op | source)
XLA Modules:
  0.0 71.4 jit_solution(5123657337619987184)
XLA Ops:
  0.0 0.5 collective-permute-start
  0.5 4.0 %collective-permute-start.3 = (bf16[128,1024]{1,0:T(8,128)(2,1)}, bf16[128,1024]{1,0:T(8,128)(2,1)S(1)}, u32[]{:S(2)}, u32[]{:S(2)}) collective-permute-start(bf16[128,1024]{1,0:T(8,128)(2,1)} %param.2), channel_id=1, source_target_pairs={{4,0},{8,4},{12,8},{16,12},{20,16},{24,20},{28,24},{0,28},{5,1},{9... | collective-permute-start | bytes 786440 | tf_op jit(solution)/shard_map/ppermute | solution.py:13
  4.5 4.5 %collective-permute-done = bf16[128,1024]{1,0:T(8,128)(2,1)S(1)} collective-permute-done((bf16[128,1024]{1,0:T(8,128)(2,1)}, bf16[128,1024]{1,0:T(8,128)(2,1)S(1)}, u32[]{:S(2)}, u32[]{:S(2)}) %collective-permute-start) | collective-permute-done | bytes 262176 | tf_op jit(solution)/shard_map/ppermute | solution.py:13
  9.0 0.0 collective-permute-start.1
  9.0 0.7 subtract_bitcast_fusion
  9.7 0.0 collective-permute-done.3
  9.7 3.5 %collective-permute-start.4 = (bf16[128,1024]{1,0:T(8,128)(2,1)S(1)}, bf16[128,1024]{1,0:T(8,128)(2,1)S(1)}, u32[]{:S(2)}, u32[]{:S(2)}) collective-permute-start(bf16[128,1024]{1,0:T(8,128)(2,1)S(1)} %collective-permute-done.3), channel_id=1, source_target_pairs={{4,0},{8,4},{12,8},{16,12},{20,16},{24,20},{28,24},{0,28},{5,1},{9... | collective-permute-start | bytes 786440 | tf_op jit(solution)/shard_map/ppermute | solution.py:13
  13.2 3.5 %collective-permute-done.1 = bf16[128,1024]{1,0:T(8,128)(2,1)S(1)} collective-permute-done((bf16[128,1024]{1,0:T(8,128)(2,1)S(1)}, bf16[128,1024]{1,0:T(8,128)(2,1)S(1)}, u32[]{:S(2)}, u32[]{:S(2)}) %collective-permute-start.1) | collective-permute-done | bytes 262176 | tf_op jit(solution)/shard_map/ppermute | solution.py:13
  16.7 1.1 %fusion.56 = f32[8,1024]{1,0:T(8,128)S(1)} fusion(bf16[128,1024]{1,0:T(8,128)(2,1)} %param.2, s32[8]{0:T(128)S(1)} %subtract_bitcast_fusion), kind=kOutput, calls=%fused_computation.66 | convolution fusion | flops 2098176 | bytes 294944 | tf_op jit(solution)/shard_map/dot_general | solution.py:28
  17.8 1.0 %convert_element_type.21 = f32[128,1024]{1,0:T(8,128)S(1)} convert(bf16[128,1024]{1,0:T(8,128)(2,1)} %param.2) | non-fusion elementwise | flops 131072 | bytes 786432 | tf_op jit(solution)/shard_map/convert_element_type | solution.py:32
  18.8 29.4 %psum.7 = f32[8,1024]{1,0:T(8,128)S(1)} all-reduce(f32[8,1024]{1,0:T(8,128)S(1)} %fusion.56), channel_id=1, replica_groups=mesh['vec'=8,'rep'=4] {'vec'}, use_global_device_ids=true, to_apply=%region_0.0 | all-reduce | flops 8192 | bytes 65536 | tf_op jit(solution)/shard_map/psum | solution.py:29
  48.3 0.1 reduce_sum.9
  48.4 0.0 collective-permute-done.4
  48.4 0.1 collective-permute-start.5
  48.5 0.0 collective-permute-done.2
  48.5 1.0 %fusion.41 = f32[7,32,128]{2,1,0:T(8,128)S(1)} fusion(bf16[128,1024]{1,0:T(8,128)(2,1)S(1)} %collective-permute-done.2, bf16[128,1024]{1,0:T(8,128)(2,1)} %param.2, s32[]{:T(128)S(6)} %select_n.3), kind=kOutput, calls=%fused_computation.50 | convolution fusion | flops 8388607 | bytes 344068 | tf_op jit(solution)/shard_map/dot_general | solution.py:17
  49.5 1.0 %fusion.40 = f32[7,32,128]{2,1,0:T(8,128)S(1)} fusion(f32[7,32,128]{2,1,0:T(8,128)S(1)} %fusion.41, bf16[128,1024]{1,0:T(8,128)(2,1)S(1)} %collective-permute-done.1, bf16[128,1024]{1,0:T(8,128)(2,1)} %param.2, s32[]{:T(128)S(6)} %select_n.3), kind=kOutput, calls=%fused_computation.48 | convolution fusion | flops 8388608 | bytes 344068 | tf_op jit(solution)/shard_map/dot_general | solution.py:17
  50.5 1.0 %fusion.39 = f32[7,32,128]{2,1,0:T(8,128)S(1)} fusion(f32[7,32,128]{2,1,0:T(8,128)S(1)} %fusion.40, bf16[128,1024]{1,0:T(8,128)(2,1)S(1)} %collective-permute-done, bf16[128,1024]{1,0:T(8,128)(2,1)} %param.2, s32[]{:T(128)S(6)} %select_n.3), kind=kOutput, calls=%fused_computation.46 | convolution fusion | flops 8388608 | bytes 344068 | tf_op jit(solution)/shard_map/dot_general | solution.py:17
  51.6 1.2 %fusion.38 = f32[7,32,128]{2,1,0:T(8,128)S(1)} fusion(f32[7,32,128]{2,1,0:T(8,128)S(1)} %fusion.39, bf16[128,1024]{1,0:T(8,128)(2,1)} %param.2, s32[]{:T(128)S(6)} %select_n.3), kind=kOutput, calls=%fused_computation.44 | convolution fusion | flops 8388608 | bytes 344068 | tf_op jit(solution)/shard_map/dot_general | solution.py:17
  52.8 0.7 %fusion.22 = f32[7,8,128,128]{3,2,1,0:T(8,128)S(1)} fusion(f32[8,1024]{1,0:T(8,128)S(1)} %psum.7, f32[128,1024]{1,0:T(8,128)S(1)} %convert_element_type.21, bf16[128,1024]{1,0:T(8,128)(2,1)S(1)} %collective-permute-done.2), kind=kOutput, calls=%fused_computation.24 | convolution fusion | flops 270532608 | bytes 1343488 | tf_op jit(solution)/shard_map/dot_general | solution.py:17
  53.6 0.7 fusion.24
  54.3 0.7 fusion.26
  55.0 0.2 fusion.37
  55.2 0.2 fusion.36
  55.4 0.7 %fusion.28 = f32[7,8,128,128]{3,2,1,0:T(8,128)S(1)} fusion(f32[7,8,128,128]{3,2,1,0:T(8,128)S(1)} %fusion.26, f32[8,1024]{1,0:T(8,128)S(1)} %psum.7, f32[128,1024]{1,0:T(8,128)S(1)} %convert_element_type.21, bf16[128,1024]{1,0:T(8,128)(2,1)S(1)} %copy-done), kind=kOutput, calls=%fused_computation.30 | convolution fusion | flops 270532608 | bytes 1343488 | tf_op jit(solution)/shard_map/dot_general | solution.py:17
  56.1 0.0 collective-permute-done.5
  56.1 0.2 fusion.35
  56.3 11.0 %all_gather.3 = f32[7,128,128]{2,1,0:T(8,128)S(1)} all-gather(f32[7,32,128]{2,1,0:T(8,128)S(1)} %fusion.35), channel_id=1, replica_groups=mesh['vec'=8,'rep'=4] {'rep'}, dimensions={1}, use_global_device_ids=true | all-gather | bytes 573440 | tf_op jit(solution)/shard_map/all_gather | solution.py:53
  67.3 0.7 fusion.30
  68.0 0.7 fusion.32
  68.8 0.7 fusion.34
  69.5 1.9 %multiply_convert_fusion.8 = bf16[7,8,128,128]{3,2,1,0:T(8,128)(2,1)} fusion(f32[7,8,128,128]{3,2,1,0:T(8,128)S(1)} %fusion.34, f32[7,128,128]{2,1,0:T(8,128)S(1)} %all_gather.3, f32[8]{0:T(128)S(1)} %broadcast_multiply_fusion), kind=kLoop, calls=%fused_computation.8 | loop fusion | flops 3670016 | bytes 5963808 | tf_op jit(solution)/shard_map/convert_element_type | solution.py:57
  (4 shorter events, 0.0 us)
Async XLA Ops:
  0.0 9.0 %collective-permute-start = (bf16[128,1024]{1,0:T(8,128)(2,1)}, bf16[128,1024]{1,0:T(8,128)(2,1)S(1)}, u32[]{:S(2)}, u32[]{:S(2)}) collective-permute-start(bf16[128,1024]{1,0:T(8,128)(2,1)} %param.2), channel_id=1, source_target_pairs={{28,0},{0,4},{4,8},{8,12},{12,16},{16,20},{20,24},{24,28},{29,1},{... | collective-permute-start | bytes 786440 | tf_op jit(solution)/shard_map/ppermute | solution.py:13
  0.5 9.2 %collective-permute-start.3 = (bf16[128,1024]{1,0:T(8,128)(2,1)}, bf16[128,1024]{1,0:T(8,128)(2,1)S(1)}, u32[]{:S(2)}, u32[]{:S(2)}) collective-permute-start(bf16[128,1024]{1,0:T(8,128)(2,1)} %param.2), channel_id=1, source_target_pairs={{4,0},{8,4},{12,8},{16,12},{20,16},{24,20},{28,24},{0,28},{5,1},{9... | collective-permute-start | bytes 786440 | tf_op jit(solution)/shard_map/ppermute | solution.py:13
  9.0 7.7 %collective-permute-start.1 = (bf16[128,1024]{1,0:T(8,128)(2,1)S(1)}, bf16[128,1024]{1,0:T(8,128)(2,1)S(1)}, u32[]{:S(2)}, u32[]{:S(2)}) collective-permute-start(bf16[128,1024]{1,0:T(8,128)(2,1)S(1)} %collective-permute-done), channel_id=1, source_target_pairs={{28,0},{0,4},{4,8},{8,12},{12,16},{16,20},{20,24},{24,28},{29,1},{... | collective-permute-start | bytes 786440 | tf_op jit(solution)/shard_map/ppermute | solution.py:13
  9.7 38.7 %collective-permute-start.4 = (bf16[128,1024]{1,0:T(8,128)(2,1)S(1)}, bf16[128,1024]{1,0:T(8,128)(2,1)S(1)}, u32[]{:S(2)}, u32[]{:S(2)}) collective-permute-start(bf16[128,1024]{1,0:T(8,128)(2,1)S(1)} %collective-permute-done.3), channel_id=1, source_target_pairs={{4,0},{8,4},{12,8},{16,12},{20,16},{24,20},{28,24},{0,28},{5,1},{9... | collective-permute-start | bytes 786440 | tf_op jit(solution)/shard_map/ppermute | solution.py:13
  16.7 31.8 %collective-permute-start.2 = (bf16[128,1024]{1,0:T(8,128)(2,1)S(1)}, bf16[128,1024]{1,0:T(8,128)(2,1)S(1)}, u32[]{:S(2)}, u32[]{:S(2)}) collective-permute-start(bf16[128,1024]{1,0:T(8,128)(2,1)S(1)} %collective-permute-done.1), channel_id=1, source_target_pairs={{28,0},{0,4},{4,8},{8,12},{12,16},{16,20},{20,24},{24,28},{29,1},{... | collective-permute-start | bytes 786440 | tf_op jit(solution)/shard_map/ppermute | solution.py:13
  48.4 7.7 %collective-permute-start.5 = (bf16[128,1024]{1,0:T(8,128)(2,1)S(1)}, bf16[128,1024]{1,0:T(8,128)(2,1)S(1)}, u32[]{:S(2)}, u32[]{:S(2)}) collective-permute-start(bf16[128,1024]{1,0:T(8,128)(2,1)S(1)} %collective-permute-done.4), channel_id=1, source_target_pairs={{4,0},{8,4},{12,8},{16,12},{20,16},{24,20},{28,24},{0,28},{5,1},{9... | collective-permute-start | bytes 786440 | tf_op jit(solution)/shard_map/ppermute | solution.py:13
  52.8 2.2 %copy-start = (bf16[128,1024]{1,0:T(8,128)(2,1)S(1)}, bf16[128,1024]{1,0:T(8,128)(2,1)}, u32[]{:S(2)}) copy-start(bf16[128,1024]{1,0:T(8,128)(2,1)} %param.2) | copy-start | bytes 786436
where the time goes:
time: 71.7 us; the launch traced here: 71.4 us
  blocking collectives  40.5 us (56%)
  matrix products  11 us (15%)
  starting transfers between devices  8.13 us (11%)
  waiting for transfers between devices  7.96 us (11%)
  other arithmetic  3.69 us (5%)
    psum x1, blocking collectives, on_device(): pivots = lax.psum(local_rows, 'vec')  29.4 us
    all_gather x1, blocking collectives, on_device(): gram_all = lax.all_gather(gram_all, 'rep', axis=1, tiled=True)  11 us
    dot_general x14, matrix products, contract(): lax.dot_general(left, right, (((1,), (1,)), ((), ())), preferred_element_...  9.87 us
    ppermute x6, starting transfers between devices, from_behind(): return lax.ppermute(block, axis, route)  8.13 us
    ppermute x6, waiting for transfers between devices, from_behind(): return lax.ppermute(block, axis, route)  7.96 us
    convert_element_type x1, other arithmetic, on_device(): return similarity.astype(jnp.bfloat16)  1.9 us
  transfers between devices with their start and end apart: 6, of which 2 were waited for; matrix products, arithmetic and copies ran while one was open for 15% of the time, Pallas kernels for 0%

commit v1 on v0

--- a/solution.py
+++ b/solution.py
@@ -50,7 +50,9 @@
         grams[HALF + reach] = contract(own_rows, upper)
     triple_all = jnp.stack(triples).reshape(window, count, block_rows, block_rows)
     gram_all = jnp.stack(grams)
-    gram_all = lax.all_gather(gram_all, "rep", axis=1, tiled=True)
+    gram_all = jnp.concatenate(
+        lax.all_to_all(jnp.stack([gram_all] * lax.axis_size("rep")), "rep", 0, 0), axis=1
+    )
     similarity = (triple_all - centre[None, :, None, None] * gram_all[:, None, :, :]) / math.sqrt(
         fields
     )

time: 71.7 us -> 75.8 us (1.057)
  blocking collectives: 40.5 us -> 29.4 us
  starting transfers between devices: 8.13 us -> 12.8 us
  waiting for transfers between devices: 7.96 us -> 11.4 us
  local copies, waits for them, and re-layouts: 0.01 us -> 2.45 us
  matrix products: 11 us -> 13.4 us
  other arithmetic: 3.69 us -> 5.72 us
    all_gather x1 -> x0, blocking collectives: 11 us -> none  [on_device(): gram_all = lax.all_gather(gram_all, 'rep', axis=1, tiled=True)]
    all_to_all x0 -> x1, starting transfers between devices: none -> 4.67 us  [on_device(): lax.all_to_all(jnp.stack([gram_all] * lax.axis_size('rep')), 'rep', 0, 0)]
    all_to_all x0 -> x1, waiting for transfers between devices: none -> 3.45 us  [on_device(): lax.all_to_all(jnp.stack([gram_all] * lax.axis_size('rep')), 'rep', 0, 0)]
    dot_general x14, matrix products: 9.87 us -> 12.3 us  [contract(): lax.dot_general(left, right, (((1,), (1,)), ((), ())), preferred_element_...]
    convert_element_type x1, other arithmetic: 1.9 us -> 3.93 us  [on_device(): return similarity.astype(jnp.bfloat16)]
    unnamed x2 -> x4, local copies, waits for them, and re-layouts: 0.01 us -> 1.6 us
    another operation x0 -> x1, local copies, waits for them, and re-layouts: none -> 0.82 us  [on_device(): jnp.stack([gram_all] * lax.axis_size('rep'))]
  transfers between devices with their start and end apart: 6 -> 7, of which waited for: 2 -> 3; matrix products, arithmetic and copies ran while one was open for 15% -> 20% of each run, Pallas kernels for 0% -> 0%
where the time goes in v1:
time: 75.8 us; the launch traced here: 75.3 us
  blocking collectives  29.4 us (39%)
  matrix products  13.4 us (18%)
  starting transfers between devices  12.8 us (17%)
  waiting for transfers between devices  11.4 us (15%)
  other arithmetic  5.72 us (8%)
  local copies, waits for them, and re-layouts  2.45 us (3%)
    psum x1, blocking collectives, on_device(): pivots = lax.psum(local_rows, 'vec')  29.4 us
    dot_general x14, matrix products, contract(): lax.dot_general(left, right, (((1,), (1,)), ((), ())), preferred_element_...  12.3 us
    ppermute x6, starting transfers between devices, from_behind(): return lax.ppermute(block, axis, route)  8.13 us
    ppermute x6, waiting for transfers between devices, from_behind(): return lax.ppermute(block, axis, route)  7.96 us
    all_to_all x1, starting transfers between devices, on_device(): lax.all_to_all(jnp.stack([gram_all] * lax.axis_size('rep')), 'rep', 0, 0)  4.67 us
    convert_element_type x1, other arithmetic, on_device(): return similarity.astype(jnp.bfloat16)  3.93 us
    all_to_all x1, waiting for transfers between devices, on_device(): lax.all_to_all(jnp.stack([gram_all] * lax.axis_size('rep')), 'rep', 0, 0)  3.45 us
    unnamed x4, local copies, waits for them, and re-layouts  1.6 us
  transfers between devices with their start and end apart: 7, of which 3 were waited for; matrix products, arithmetic and copies ran while one was open for 20% of the time, Pallas kernels for 0%

profile of v1, /device:TPU:0, one launch (start us, length us, event | category | flops | bytes accessed | tf_op | source)
XLA Modules:
  0.0 75.3 jit_solution(11866600567068199172)
XLA Ops:
  0.0 0.5 collective-permute-start
  0.5 4.0 %collective-permute-start.3 = (bf16[128,1024]{1,0:T(8,128)(2,1)}, bf16[128,1024]{1,0:T(8,128)(2,1)S(1)}, u32[]{:S(2)}, u32[]{:S(2)}) collective-permute-start(bf16[128,1024]{1,0:T(8,128)(2,1)} %param.2), channel_id=1, source_target_pairs={{4,0},{8,4},{12,8},{16,12},{20,16},{24,20},{28,24},{0,28},{5,1},{9... | collective-permute-start | bytes 786440 | tf_op jit(solution)/shard_map/ppermute | solution.py:13
  4.5 4.5 %collective-permute-done = bf16[128,1024]{1,0:T(8,128)(2,1)S(1)} collective-permute-done((bf16[128,1024]{1,0:T(8,128)(2,1)}, bf16[128,1024]{1,0:T(8,128)(2,1)S(1)}, u32[]{:S(2)}, u32[]{:S(2)}) %collective-permute-start) | collective-permute-done | bytes 262176 | tf_op jit(solution)/shard_map/ppermute | solution.py:13
  9.0 0.7 subtract_bitcast_fusion
  9.7 0.0 collective-permute-done.3
  9.7 3.5 %collective-permute-start.4 = (bf16[128,1024]{1,0:T(8,128)(2,1)S(1)}, bf16[128,1024]{1,0:T(8,128)(2,1)S(1)}, u32[]{:S(2)}, u32[]{:S(2)}) collective-permute-start(bf16[128,1024]{1,0:T(8,128)(2,1)S(1)} %collective-permute-done.3), channel_id=1, source_target_pairs={{4,0},{8,4},{12,8},{16,12},{20,16},{24,20},{28,24},{0,28},{5,1},{9... | collective-permute-start | bytes 786440 | tf_op jit(solution)/shard_map/ppermute | solution.py:13
  13.2 3.5 %collective-permute-done.1 = bf16[128,1024]{1,0:T(8,128)(2,1)S(1)} collective-permute-done((bf16[128,1024]{1,0:T(8,128)(2,1)S(1)}, bf16[128,1024]{1,0:T(8,128)(2,1)S(1)}, u32[]{:S(2)}, u32[]{:S(2)}) %collective-permute-start.1) | collective-permute-done | bytes 262176 | tf_op jit(solution)/shard_map/ppermute | solution.py:13
  16.7 1.1 %fusion.56 = f32[8,1024]{1,0:T(8,128)S(1)} fusion(bf16[128,1024]{1,0:T(8,128)(2,1)} %param.2, s32[8]{0:T(128)S(1)} %subtract_bitcast_fusion), kind=kOutput, calls=%fused_computation.66 | convolution fusion | flops 2098176 | bytes 294944 | tf_op jit(solution)/shard_map/dot_general | solution.py:28
  17.8 1.0 %convert_element_type.21 = f32[128,1024]{1,0:T(8,128)S(1)} convert(bf16[128,1024]{1,0:T(8,128)(2,1)} %param.2) | non-fusion elementwise | flops 131072 | bytes 786432 | tf_op jit(solution)/shard_map/convert_element_type | solution.py:32
  18.8 29.4 %psum.7 = f32[8,1024]{1,0:T(8,128)S(1)} all-reduce(f32[8,1024]{1,0:T(8,128)S(1)} %fusion.56), channel_id=1, replica_groups=mesh['vec'=8,'rep'=4] {'vec'}, use_global_device_ids=true, to_apply=%region_0.0 | all-reduce | flops 8192 | bytes 65536 | tf_op jit(solution)/shard_map/psum | solution.py:29
  48.3 0.1 reduce_sum.9
  48.4 0.0 collective-permute-done.4
  48.4 0.1 collective-permute-start.5
  48.5 1.0 %fusion.41 = f32[7,32,128]{2,1,0:T(8,128)S(1)} fusion(bf16[128,1024]{1,0:T(8,128)(2,1)S(1)} %collective-permute-done.2, bf16[128,1024]{1,0:T(8,128)(2,1)} %param.2, s32[]{:T(128)S(6)} %select_n.3), kind=kOutput, calls=%fused_computation.50 | convolution fusion | flops 8388607 | bytes 344068 | tf_op jit(solution)/shard_map/dot_general | solution.py:17
  49.5 1.0 %fusion.40 = f32[7,32,128]{2,1,0:T(8,128)S(1)} fusion(f32[7,32,128]{2,1,0:T(8,128)S(1)} %fusion.41, bf16[128,1024]{1,0:T(8,128)(2,1)S(1)} %collective-permute-done.1, bf16[128,1024]{1,0:T(8,128)(2,1)} %param.2, s32[]{:T(128)S(6)} %select_n.3), kind=kOutput, calls=%fused_computation.48 | convolution fusion | flops 8388608 | bytes 344068 | tf_op jit(solution)/shard_map/dot_general | solution.py:17
  50.5 1.0 %fusion.39 = f32[7,32,128]{2,1,0:T(8,128)S(1)} fusion(f32[7,32,128]{2,1,0:T(8,128)S(1)} %fusion.40, bf16[128,1024]{1,0:T(8,128)(2,1)S(1)} %collective-permute-done, bf16[128,1024]{1,0:T(8,128)(2,1)} %param.2, s32[]{:T(128)S(6)} %select_n.3), kind=kOutput, calls=%fused_computation.46 | convolution fusion | flops 8388608 | bytes 344068 | tf_op jit(solution)/shard_map/dot_general | solution.py:17
  51.6 1.2 %fusion.38 = f32[7,32,128]{2,1,0:T(8,128)S(1)} fusion(f32[7,32,128]{2,1,0:T(8,128)S(1)} %fusion.39, bf16[128,1024]{1,0:T(8,128)(2,1)} %param.2, s32[]{:T(128)S(6)} %select_n.3), kind=kOutput, calls=%fused_computation.44 | convolution fusion | flops 8388608 | bytes 344068 | tf_op jit(solution)/shard_map/dot_general | solution.py:17
  52.8 0.7 fusion.22
  53.6 0.7 fusion.24
  54.3 0.7 fusion.26
  55.0 0.2 fusion.37
  55.2 0.2 fusion.36
  55.4 0.7 fusion.28
  56.1 0.2 fusion.35
  56.3 1.6 %copy-done.1 = f32[7,8,128,128]{3,2,1,0:T(8,128)} copy-done((f32[7,8,128,128]{3,2,1,0:T(8,128)}, f32[7,8,128,128]{3,2,1,0:T(8,128)S(1)}, u32[]{:S(2)}) %copy-start.1) | copy-done | bytes 3670040
  57.9 0.8 %stack.50 = f32[4,7,32,128]{3,2,1,0:T(8,128)} broadcast(f32[7,32,128]{2,1,0:T(8,128)S(1)} %fusion.35), dimensions={1,2,3} | broadcast | bytes 573440 | tf_op jit(solution)/shard_map/stack | solution.py:54
  58.7 4.7 %all-to-all-start = ((f32[4,7,32,128]{3,2,1,0:T(8,128)}), f32[4,7,32,128]{3,2,1,0:T(8,128)S(1)}, u32[]{:S(2)}, u32[]{:S(2)}) async-start(f32[4,7,32,128]{3,2,1,0:T(8,128)} %stack.50), calls=%async_computation | async-start | bytes 917504 | tf_op jit(solution)/shard_map/all_to_all | solution.py:54
  63.4 1.5 %fusion.30 = f32[7,8,128,128]{3,2,1,0:T(8,128)} fusion(f32[7,8,128,128]{3,2,1,0:T(8,128)} %copy-done.1, f32[8,1024]{1,0:T(8,128)S(1)} %psum.7, f32[128,1024]{1,0:T(8,128)S(1)} %convert_element_type.21, bf16[128,1024]{1,0:T(8,128)(2,1)S(1)} %collective-permute-done.3), kind=kOutput, calls=%fused_computation.32 | convolution fusion | flops 270532608 | bytes 1343488 | tf_op jit(solution)/shard_map/dot_general | solution.py:17
  64.9 1.5 %fusion.32 = f32[7,8,128,128]{3,2,1,0:T(8,128)} fusion(f32[7,8,128,128]{3,2,1,0:T(8,128)} %fusion.30, f32[8,1024]{1,0:T(8,128)S(1)} %psum.7, f32[128,1024]{1,0:T(8,128)S(1)} %convert_element_type.21, bf16[128,1024]{1,0:T(8,128)(2,1)S(1)} %collective-permute-done.4), kind=kOutput, calls=%fused_computation.34 | convolution fusion | flops 270532608 | bytes 1343488 | tf_op jit(solution)/shard_map/dot_general | solution.py:17
  66.4 1.5 %fusion.34 = f32[7,8,128,128]{3,2,1,0:T(8,128)} fusion(f32[7,8,128,128]{3,2,1,0:T(8,128)} %fusion.32, f32[8,1024]{1,0:T(8,128)S(1)} %psum.7, f32[128,1024]{1,0:T(8,128)S(1)} %convert_element_type.21, bf16[128,1024]{1,0:T(8,128)(2,1)S(1)} %collective-permute-done.5), kind=kOutput, calls=%fused_computation.36 | convolution fusion | flops 270532608 | bytes 1343488 | tf_op jit(solution)/shard_map/dot_general | solution.py:17
  67.9 3.4 %all-to-all-done = f32[4,7,32,128]{3,2,1,0:T(8,128)S(1)} async-done(((f32[4,7,32,128]{3,2,1,0:T(8,128)}), f32[4,7,32,128]{3,2,1,0:T(8,128)S(1)}, u32[]{:S(2)}, u32[]{:S(2)}) %all-to-all-start) | async-done | bytes 458784 | tf_op jit(solution)/shard_map/all_to_all | solution.py:54
  71.4 3.9 %multiply_convert_fusion.8 = bf16[7,8,128,128]{3,2,1,0:T(8,128)(2,1)} fusion(f32[7,8,128,128]{3,2,1,0:T(8,128)} %fusion.34, f32[7,128,128]{2,1,0:T(8,128)S(1)} %bitcast.90, f32[8]{0:T(128)S(1)} %broadcast_multiply_fusion), kind=kLoop, calls=%fused_computation.8 | loop fusion | flops 3670016 | bytes 5963808 | tf_op jit(solution)/shard_map/convert_element_type | solution.py:59
  (9 shorter events, 0.1 us)
Async XLA Ops:
  0.0 9.0 %collective-permute-start = (bf16[128,1024]{1,0:T(8,128)(2,1)}, bf16[128,1024]{1,0:T(8,128)(2,1)S(1)}, u32[]{:S(2)}, u32[]{:S(2)}) collective-permute-start(bf16[128,1024]{1,0:T(8,128)(2,1)} %param.2), channel_id=1, source_target_pairs={{28,0},{0,4},{4,8},{8,12},{12,16},{16,20},{20,24},{24,28},{29,1},{... | collective-permute-start | bytes 786440 | tf_op jit(solution)/shard_map/ppermute | solution.py:13
  0.5 9.2 %collective-permute-start.3 = (bf16[128,1024]{1,0:T(8,128)(2,1)}, bf16[128,1024]{1,0:T(8,128)(2,1)S(1)}, u32[]{:S(2)}, u32[]{:S(2)}) collective-permute-start(bf16[128,1024]{1,0:T(8,128)(2,1)} %param.2), channel_id=1, source_target_pairs={{4,0},{8,4},{12,8},{16,12},{20,16},{24,20},{28,24},{0,28},{5,1},{9... | collective-permute-start | bytes 786440 | tf_op jit(solution)/shard_map/ppermute | solution.py:13
  9.0 7.7 %collective-permute-start.1 = (bf16[128,1024]{1,0:T(8,128)(2,1)S(1)}, bf16[128,1024]{1,0:T(8,128)(2,1)S(1)}, u32[]{:S(2)}, u32[]{:S(2)}) collective-permute-start(bf16[128,1024]{1,0:T(8,128)(2,1)S(1)} %collective-permute-done), channel_id=1, source_target_pairs={{28,0},{0,4},{4,8},{8,12},{12,16},{16,20},{20,24},{24,28},{29,1},{... | collective-permute-start | bytes 786440 | tf_op jit(solution)/shard_map/ppermute | solution.py:13
  9.7 38.7 %collective-permute-start.4 = (bf16[128,1024]{1,0:T(8,128)(2,1)S(1)}, bf16[128,1024]{1,0:T(8,128)(2,1)S(1)}, u32[]{:S(2)}, u32[]{:S(2)}) collective-permute-start(bf16[128,1024]{1,0:T(8,128)(2,1)S(1)} %collective-permute-done.3), channel_id=1, source_target_pairs={{4,0},{8,4},{12,8},{16,12},{20,16},{24,20},{28,24},{0,28},{5,1},{9... | collective-permute-start | bytes 786440 | tf_op jit(solution)/shard_map/ppermute | solution.py:13
  16.7 31.8 %collective-permute-start.2 = (bf16[128,1024]{1,0:T(8,128)(2,1)S(1)}, bf16[128,1024]{1,0:T(8,128)(2,1)S(1)}, u32[]{:S(2)}, u32[]{:S(2)}) collective-permute-start(bf16[128,1024]{1,0:T(8,128)(2,1)S(1)} %collective-permute-done.1), channel_id=1, source_target_pairs={{28,0},{0,4},{4,8},{8,12},{12,16},{16,20},{20,24},{24,28},{29,1},{... | collective-permute-start | bytes 786440 | tf_op jit(solution)/shard_map/ppermute | solution.py:13
  48.4 7.7 %collective-permute-start.5 = (bf16[128,1024]{1,0:T(8,128)(2,1)S(1)}, bf16[128,1024]{1,0:T(8,128)(2,1)S(1)}, u32[]{:S(2)}, u32[]{:S(2)}) collective-permute-start(bf16[128,1024]{1,0:T(8,128)(2,1)S(1)} %collective-permute-done.4), channel_id=1, source_target_pairs={{4,0},{8,4},{12,8},{16,12},{20,16},{24,20},{28,24},{0,28},{5,1},{9... | collective-permute-start | bytes 786440 | tf_op jit(solution)/shard_map/ppermute | solution.py:13
  52.8 2.2 %copy-start = (bf16[128,1024]{1,0:T(8,128)(2,1)S(1)}, bf16[128,1024]{1,0:T(8,128)(2,1)}, u32[]{:S(2)}) copy-start(bf16[128,1024]{1,0:T(8,128)(2,1)} %param.2) | copy-start | bytes 786436
  56.1 1.8 %copy-start.1 = (f32[7,8,128,128]{3,2,1,0:T(8,128)}, f32[7,8,128,128]{3,2,1,0:T(8,128)S(1)}, u32[]{:S(2)}) copy-start(f32[7,8,128,128]{3,2,1,0:T(8,128)S(1)} %fusion.28) | copy-start | bytes 11010052
  58.7 12.6 %all-to-all-start = ((f32[4,7,32,128]{3,2,1,0:T(8,128)}), f32[4,7,32,128]{3,2,1,0:T(8,128)S(1)}, u32[]{:S(2)}, u32[]{:S(2)}) async-start(f32[4,7,32,128]{3,2,1,0:T(8,128)} %stack.50), calls=%async_computation | async-start | bytes 917504 | tf_op jit(solution)/shard_map/all_to_all | solution.py:54
